TPU v7x, 256 devices: a whole 4x4x8 slice. The times are simulated.
256 devices in a mesh: sec: 4 (over x_hi, core), ctx: 64 (over y, x_lo, z).
Axes of the slice: x: 4 (x_hi: 2, x_lo: 2; x = x_hi * 2 + x_lo), y: 4, z: 8, core: 2. Of those that a mesh axis runs over, the one named last changes fastest.
Arguments:
- queries: bfloat16 [4, 128, 64, 4096], P('sec', 'ctx'), may hold values from -6 to 6
- head_weights: float32 [4, 128, 64, 32], P('sec', 'ctx'), may hold values from -0.9 to 0.9
- key_vectors: bfloat16 [4, 524288, 128], P('sec', 'ctx'), may hold values from -6 to 6
- targets: bfloat16 [4, 128, 64, 4096], P('sec', 'ctx'), may hold values from 0 to 0.0019989014
- normalizers: float32 [4, 128, 64], P('sec', 'ctx'), may hold values from 7 to 9
- loss_grad: float32 [4, 128, 64], P('sec', 'ctx'), may hold values from 300 to 3000
- tile_slot: int32 [4, 128], P('sec', 'ctx'), may hold values from 0 to 127
- doc_start: int32 [4, 128], P('sec', 'ctx'), may hold values from 0 to 524287, as said below
Outputs:
- queries_grad: bfloat16 [4, 128, 64, 4096], P('sec', 'ctx')
- weights_grad: float32 [4, 128, 64, 32], P('sec', 'ctx')
- key_grads: bfloat16 [4, 524288, 128], P('sec', 'ctx')
Inputs may be any that keep to these rules, and one draw needn't show every extreme that they name: `doc_start`: qpos of every task lies in its device's positions; the document of a task starts at or before its first query and spans 1 to 4 key blocks up to its last query; the first task of every device but the first spans 4 blocks and its document starts on the device before.
All inputs are finite; a program needn't handle non-finite values.
Results may differ from a plain program's by a relative error of at most 0.0051.
Values may be sent and summed in bfloat16 or wider, within the bound.
A program may use at most 192 MiB of HBM per device.

v0:
```python
import jax
import jax.numpy as jnp
from jax import lax
from jax.sharding import PartitionSpec as P

BLK = 1024
MAXB = 4
QT = 64
KB_DEV = 8


def passed_along(array, axis, by):
    size = lax.axis_size(axis)
    pairs = [(i, i + by) for i in range(size) if 0 <= i + by < size]
    return lax.ppermute(array, axis, pairs)


def block_terms(
    query_rows,
    weight_rows,
    normalizer,
    cotangent,
    target_block,
    key_block,
    key_first,
    query_pos,
    doc_begin,
    inside,
):
    tile_rows = weight_rows.shape[0]
    head_count = weight_rows.shape[1]
    block_width = key_block.shape[0]
    factor = 1.0 / key_block.shape[1] ** 0.5
    scores = lax.dot_general(
        query_rows, key_block, (((1,), (1,)), ((), ())), preferred_element_type=jnp.float32
    )
    scores = scores.reshape(tile_rows, head_count, block_width)
    active = jnp.maximum(scores, 0.0) * factor
    index_value = jnp.sum(weight_rows[:, :, None] * active, axis=1)
    key_pos = key_first + jnp.arange(block_width, dtype=jnp.int32)
    live = (key_pos[None, :] >= doc_begin) & (key_pos[None, :] <= query_pos[:, None]) & inside
    delta = jnp.where(
        live,
        cotangent[:, None]
        * (jnp.exp(index_value - normalizer[:, None]) - target_block.astype(jnp.float32)),
        0.0,
    )
    weight_part = jnp.sum(delta[:, None, :] * active, axis=2)
    score_grad = jnp.where(
        scores > 0, delta[:, None, :] * weight_rows[:, :, None] * factor, 0.0
    ).astype(jnp.bfloat16)
    score_grad = score_grad.reshape(tile_rows * head_count, block_width)
    query_part = jnp.dot(score_grad, key_block, preferred_element_type=jnp.float32)
    key_part = lax.dot_general(
        score_grad, query_rows, (((0,), (0,)), ((), ())), preferred_element_type=jnp.float32
    )
    return (query_part, weight_part, key_part)


def run_task(
    query_tile,
    weight_rows,
    target_rows,
    normalizer,
    cotangent,
    query_first,
    doc_begin,
    avail_keys,
    avail_first,
    avail_blocks,
    key_padded,
):
    depth = avail_keys.shape[1]
    tile_rows = weight_rows.shape[0]
    head_count = weight_rows.shape[1]
    query_rows = query_tile.reshape(tile_rows * head_count, depth)
    query_pos = query_first + jnp.arange(tile_rows, dtype=jnp.int32)
    slot_limit = target_rows.shape[1] // BLK
    first_block = doc_begin // BLK
    block_count = (query_first + tile_rows - 1) // BLK - first_block + 1
    lower = jnp.maximum(0, avail_first - first_block)
    upper = jnp.minimum(
        jnp.minimum(block_count, slot_limit), avail_first + avail_blocks - first_block
    )

    def per_slot(slot_index, carry):
        query_total, weight_total, slot_sums = carry
        block_id = first_block + slot_index
        inside = (
            (slot_index < block_count)
            & (slot_index < slot_limit)
            & (block_id >= avail_first)
            & (block_id < avail_first + avail_blocks)
        )
        local_block = jnp.clip(block_id - avail_first, 0, avail_blocks - 1)
        key_block = lax.dynamic_slice_in_dim(avail_keys, local_block * BLK, BLK, 0)
        target_block = lax.dynamic_slice_in_dim(
            target_rows, jnp.minimum(slot_index, slot_limit - 1) * BLK, BLK, 1
        )
        query_part, weight_part, key_part = block_terms(
            query_rows,
            weight_rows,
            normalizer,
            cotangent,
            target_block,
            key_block,
            block_id * BLK,
            query_pos,
            doc_begin,
            inside,
        )
        slot_sums = lax.dynamic_update_slice_in_dim(slot_sums, key_part, slot_index * BLK, 0)
        return (query_total + query_part, weight_total + weight_part, slot_sums)

    start_state = (
        jnp.zeros((tile_rows * head_count, depth), jnp.float32),
        jnp.zeros((tile_rows, head_count), jnp.float32),
        jnp.zeros((MAXB * BLK, depth), jnp.float32),
    )
    query_total, weight_total, slot_sums = lax.fori_loop(lower, upper, per_slot, start_state)
    window_start = jnp.clip(first_block - avail_first + MAXB, 0, avail_blocks + MAXB) * BLK
    previous = lax.dynamic_slice_in_dim(key_padded, window_start, MAXB * BLK, 0)
    key_padded = lax.dynamic_update_slice_in_dim(key_padded, previous + slot_sums, window_start, 0)
    return (query_total.reshape(tile_rows, head_count * depth), weight_total, key_padded)


def local(
    queries, head_weights, key_vectors, targets, normalizers, loss_grad, tile_slot, doc_start
):
    ctx_index = lax.axis_index("ctx")
    dev_first = ctx_index * KB_DEV
    local_keys = key_vectors[0]
    depth = local_keys.shape[1]
    rim_blocks = MAXB - 1
    task_total = queries.shape[1]
    own_first = dev_first * BLK + tile_slot[0] * QT
    query_list = []
    weight_list = []
    rim_keys = passed_along(local_keys[(KB_DEV - rim_blocks) * BLK :], "ctx", 1)
    avail_keys = jnp.concatenate([rim_keys, local_keys], axis=0)
    avail_blocks = KB_DEV + rim_blocks
    key_padded = jnp.zeros(((avail_blocks + 2 * MAXB) * BLK, depth), jnp.float32)
    for task_index in range(task_total):
        query_part, weight_part, key_padded = run_task(
            queries[0, task_index],
            head_weights[0, task_index],
            targets[0, task_index],
            normalizers[0, task_index],
            loss_grad[0, task_index],
            own_first[task_index],
            doc_start[0, task_index],
            avail_keys,
            dev_first - rim_blocks,
            avail_blocks,
            key_padded,
        )
        query_list.append(query_part)
        weight_list.append(weight_part)
    key_total = key_padded[MAXB * BLK : (MAXB + avail_blocks) * BLK]
    returned = passed_along(key_total[: rim_blocks * BLK].astype(jnp.bfloat16), "ctx", -1)
    key_own = key_total[rim_blocks * BLK :]
    key_own = jnp.concatenate(
        [
            key_own[: (KB_DEV - rim_blocks) * BLK],
            key_own[(KB_DEV - rim_blocks) * BLK :] + returned.astype(jnp.float32),
        ],
        axis=0,
    )
    query_out = jnp.stack(query_list).astype(jnp.bfloat16)[None]
    weight_out = jnp.stack(weight_list)[None]
    key_out = key_own.astype(jnp.bfloat16)[None]
    return (query_out, weight_out, key_out)


def solution(mesh):
    return jax.shard_map(
        local,
        mesh=mesh,
        in_specs=(
            P("sec", "ctx", None, None),
            P("sec", "ctx", None, None),
            P("sec", "ctx", None),
            P("sec", "ctx", None, None),
            P("sec", "ctx", None),
            P("sec", "ctx", None),
            P("sec", "ctx"),
            P("sec", "ctx"),
        ),
        out_specs=(P("sec", "ctx", None, None), P("sec", "ctx", None, None), P("sec", "ctx", None)),
        check_vma=False,
    )
```

profile of v0, /device:TPU:24, one launch (start us, length us, event | category | flops | bytes accessed | tf_op | source)
XLA Modules:
  0.0 626.2 jit_solution(6291225259285564634)
XLA Ops:
  34.5 279.6 %while.35 = (s32[]{:T(128)}, f32[2048,128]{1,0:T(8,128)S(1)}, f32[64,32]{1,0:T(8,128)S(1)}, f32[4096,128]{1,0:T(8,128)}, s32[]{:T(128)}, /*index=5*/s32[]{:T(128...) while((s32[]{:T(128)}, f32[2048,128]{1,0:T(8,128)S(1)}, ...), condition=%wide.wide.region_7.8_spmd.clone, body=%wide.wide.region_4.7_spmd.clone.sunk | while | flops 1634472960 | bytes 194735712 | solution.py:120
  45.4 9.3 %copy.44 = f32[2048,1024]{1,0:T(8,128)} copy(f32[2048,1024]{0,1:T(8,128)} %maximum_bitcast_fusion.8) | data formatting | bytes 16777216 | tf_op jit(solution)/shard_map/while/body/max | solution.py:38
  77.4 9.2 %copy.46 = f32[2048,1024]{0,1:T(8,128)} copy(f32[2048,1024]{1,0:T(8,128)} %bitcast.136) | data formatting | bytes 16777216 | tf_op jit(solution)/shard_map/while/body/mul | solution.py:50
  86.6 12.0 %multiply_reduce_fusion.15 = (f32[2048]{0:T(1024)S(1)}, bf16[2048,1024]{0,1:T(8,128)(2,1)}) fusion(f32[2048,1024]{0,1:T(8,128)} %copy.45, f32[1024,2048]{1,0:T(8,128)} %copy-done, f32[2048,1024]{0,1:T(8,128)} %copy.46, f32[2048]{0:T(1024)S(1)} %get-tuple-element.938), kind=kLoop, calls=%fused_computation.19.clone.clone.1 | loop fusion | flops 16775168 | bytes 29376512 | tf_op jit(solution)/shard_map/while/body/reduce_sum | solution.py:48
  115.3 9.3 %copy.44 = f32[2048,1024]{1,0:T(8,128)} copy(f32[2048,1024]{0,1:T(8,128)} %maximum_bitcast_fusion.8) | data formatting | bytes 16777216 | tf_op jit(solution)/shard_map/while/body/max | solution.py:38
  147.3 9.2 %copy.46 = f32[2048,1024]{0,1:T(8,128)} copy(f32[2048,1024]{1,0:T(8,128)} %bitcast.136) | data formatting | bytes 16777216 | tf_op jit(solution)/shard_map/while/body/mul | solution.py:50
  156.4 12.0 %multiply_reduce_fusion.15 = (f32[2048]{0:T(1024)S(1)}, bf16[2048,1024]{0,1:T(8,128)(2,1)}) fusion(f32[2048,1024]{0,1:T(8,128)} %copy.45, f32[1024,2048]{1,0:T(8,128)} %copy-done, f32[2048,1024]{0,1:T(8,128)} %copy.46, f32[2048]{0:T(1024)S(1)} %get-tuple-element.938), kind=kLoop, calls=%fused_computation.19.clone.clone.1 | loop fusion | flops 16775168 | bytes 29376512 | tf_op jit(solution)/shard_map/while/body/reduce_sum | solution.py:48
  185.1 9.3 %copy.44 = f32[2048,1024]{1,0:T(8,128)} copy(f32[2048,1024]{0,1:T(8,128)} %maximum_bitcast_fusion.8) | data formatting | bytes 16777216 | tf_op jit(solution)/shard_map/while/body/max | solution.py:38
  217.1 9.2 %copy.46 = f32[2048,1024]{0,1:T(8,128)} copy(f32[2048,1024]{1,0:T(8,128)} %bitcast.136) | data formatting | bytes 16777216 | tf_op jit(solution)/shard_map/while/body/mul | solution.py:50
  226.3 12.0 %multiply_reduce_fusion.15 = (f32[2048]{0:T(1024)S(1)}, bf16[2048,1024]{0,1:T(8,128)(2,1)}) fusion(f32[2048,1024]{0,1:T(8,128)} %copy.45, f32[1024,2048]{1,0:T(8,128)} %copy-done, f32[2048,1024]{0,1:T(8,128)} %copy.46, f32[2048]{0:T(1024)S(1)} %get-tuple-element.938), kind=kLoop, calls=%fused_computation.19.clone.clone.1 | loop fusion | flops 16775168 | bytes 29376512 | tf_op jit(solution)/shard_map/while/body/reduce_sum | solution.py:48
  255.0 9.3 %copy.44 = f32[2048,1024]{1,0:T(8,128)} copy(f32[2048,1024]{0,1:T(8,128)} %maximum_bitcast_fusion.8) | data formatting | bytes 16777216 | tf_op jit(solution)/shard_map/while/body/max | solution.py:38
  287.0 9.2 %copy.46 = f32[2048,1024]{0,1:T(8,128)} copy(f32[2048,1024]{1,0:T(8,128)} %bitcast.136) | data formatting | bytes 16777216 | tf_op jit(solution)/shard_map/while/body/mul | solution.py:50
  296.2 12.0 %multiply_reduce_fusion.15 = (f32[2048]{0:T(1024)S(1)}, bf16[2048,1024]{0,1:T(8,128)(2,1)}) fusion(f32[2048,1024]{0,1:T(8,128)} %copy.45, f32[1024,2048]{1,0:T(8,128)} %copy-done, f32[2048,1024]{0,1:T(8,128)} %copy.46, f32[2048]{0:T(1024)S(1)} %get-tuple-element.938), kind=kLoop, calls=%fused_computation.19.clone.clone.1 | loop fusion | flops 16775168 | bytes 29376512 | tf_op jit(solution)/shard_map/while/body/reduce_sum | solution.py:48
  316.3 283.7 %while.34 = (s32[]{:T(128)}, f32[2048,128]{1,0:T(8,128)S(1)}, f32[64,32]{1,0:T(8,128)S(1)}, f32[4096,128]{1,0:T(8,128)}, s32[]{:T(128)}, /*index=5*/s32[]{:T(128...) while((s32[]{:T(128)}, f32[2048,128]{1,0:T(8,128)S(1)}, ...), condition=%wide.wide.region_3.4_spmd.clone, body=%wide.wide.region_0.3_spmd.clone.sunk | while | flops 1634472960 | bytes 194735712 | solution.py:120
  327.4 9.3 %copy.41 = f32[2048,1024]{1,0:T(8,128)} copy(f32[2048,1024]{0,1:T(8,128)} %maximum_bitcast_fusion.7) | data formatting | bytes 16777216 | tf_op jit(solution)/shard_map/while/body/max | solution.py:38
  369.5 12.0 %multiply_reduce_fusion.13 = (f32[2048]{0:T(1024)S(1)}, bf16[2048,1024]{0,1:T(8,128)(2,1)}) fusion(f32[2048,1024]{0,1:T(8,128)} %copy.42, f32[1024,2048]{1,0:T(8,128)} %copy-done.1, f32[2048,1024]{0,1:T(8,128)} %copy.43, f32[2048]{0:T(1024)S(1)} %get-tuple-element.1016), kind=kLoop, calls=%fused_computation.2.clone.clone.1 | loop fusion | flops 16775168 | bytes 29376512 | tf_op jit(solution)/shard_map/while/body/reduce_sum | solution.py:48
  398.3 9.3 %copy.41 = f32[2048,1024]{1,0:T(8,128)} copy(f32[2048,1024]{0,1:T(8,128)} %maximum_bitcast_fusion.7) | data formatting | bytes 16777216 | tf_op jit(solution)/shard_map/while/body/max | solution.py:38
  440.4 12.0 %multiply_reduce_fusion.13 = (f32[2048]{0:T(1024)S(1)}, bf16[2048,1024]{0,1:T(8,128)(2,1)}) fusion(f32[2048,1024]{0,1:T(8,128)} %copy.42, f32[1024,2048]{1,0:T(8,128)} %copy-done.1, f32[2048,1024]{0,1:T(8,128)} %copy.43, f32[2048]{0:T(1024)S(1)} %get-tuple-element.1016), kind=kLoop, calls=%fused_computation.2.clone.clone.1 | loop fusion | flops 16775168 | bytes 29376512 | tf_op jit(solution)/shard_map/while/body/reduce_sum | solution.py:48
  469.2 9.3 %copy.41 = f32[2048,1024]{1,0:T(8,128)} copy(f32[2048,1024]{0,1:T(8,128)} %maximum_bitcast_fusion.7) | data formatting | bytes 16777216 | tf_op jit(solution)/shard_map/while/body/max | solution.py:38
  511.3 12.0 %multiply_reduce_fusion.13 = (f32[2048]{0:T(1024)S(1)}, bf16[2048,1024]{0,1:T(8,128)(2,1)}) fusion(f32[2048,1024]{0,1:T(8,128)} %copy.42, f32[1024,2048]{1,0:T(8,128)} %copy-done.1, f32[2048,1024]{0,1:T(8,128)} %copy.43, f32[2048]{0:T(1024)S(1)} %get-tuple-element.1016), kind=kLoop, calls=%fused_computation.2.clone.clone.1 | loop fusion | flops 16775168 | bytes 29376512 | tf_op jit(solution)/shard_map/while/body/reduce_sum | solution.py:48
  540.0 9.3 %copy.41 = f32[2048,1024]{1,0:T(8,128)} copy(f32[2048,1024]{0,1:T(8,128)} %maximum_bitcast_fusion.7) | data formatting | bytes 16777216 | tf_op jit(solution)/shard_map/while/body/max | solution.py:38
  572.9 9.2 %copy.43 = f32[2048,1024]{0,1:T(8,128)} copy(f32[2048,1024]{1,0:T(8,128)} %bitcast.138) | data formatting | bytes 16777216 | tf_op jit(solution)/shard_map/while/body/mul | solution.py:50
  582.1 12.0 %multiply_reduce_fusion.13 = (f32[2048]{0:T(1024)S(1)}, bf16[2048,1024]{0,1:T(8,128)(2,1)}) fusion(f32[2048,1024]{0,1:T(8,128)} %copy.42, f32[1024,2048]{1,0:T(8,128)} %copy-done.1, f32[2048,1024]{0,1:T(8,128)} %copy.43, f32[2048]{0:T(1024)S(1)} %get-tuple-element.1016), kind=kLoop, calls=%fused_computation.2.clone.clone.1 | loop fusion | flops 16775168 | bytes 29376512 | tf_op jit(solution)/shard_map/while/body/reduce_sum | solution.py:48
  613.6 9.3 %collective-permute-done.1 = bf16[3072,128]{1,0:T(8,128)(2,1)} collective-permute-done((bf16[3072,128]{1,0:T(8,128)(2,1)}, bf16[3072,128]{1,0:T(8,128)(2,1)}, u32[]{:S(2)}, u32[]{:S(2)}) %collective-permute-start.1) | collective-permute-done | bytes 786464 | tf_op jit(solution)/shard_map/ppermute | solution.py:15
  (225 shorter events, 392.2 us)
Async XLA Ops:
  0.6 19.3 %copy-start.18 = (f32[1,2,64]{2,1,0:T(2,128)S(1)}, f32[1,2,64]{2,1,0:T(2,128)}, u32[]{:S(2)}) copy-start(f32[1,2,64]{2,1,0:T(2,128)} %param.17) | copy-start | bytes 1540
  0.6 19.3 %copy-start.17 = (f32[1,2,64]{2,1,0:T(2,128)S(1)}, f32[1,2,64]{2,1,0:T(2,128)}, u32[]{:S(2)}) copy-start(f32[1,2,64]{2,1,0:T(2,128)} %param.16) | copy-start | bytes 1540
  2.7 26.7 %collective-permute-start = (bf16[3072,128]{1,0:T(8,128)(2,1)}, bf16[3072,128]{1,0:T(8,128)(2,1)}, u32[]{:S(2)}, u32[]{:S(2)}) collective-permute-start(bf16[3072,128]{1,0:T(8,128)(2,1)} %slice_bitcast_fusion.1), channel_id=1, source_target_pairs={{0,1},{1,2},{2,3},{3,4},{4,5},{5,6},{6,7},{7,8},{8,9},{9,10},{10,1... | collective-permute-start | bytes 2359304 | tf_op jit(solution)/shard_map/ppermute | solution.py:15
  34.5 281.8 %copy-start.7 = (bf16[2048,128]{1,0:T(8,128)(2,1)S(1)}, bf16[2048,128]{1,0:T(8,128)(2,1)}, u32[]{:S(2)}) copy-start(bf16[2048,128]{1,0:T(8,128)(2,1)} %reshape_squeeze.6) | copy-start | bytes 1572868
  34.5 281.8 %copy-start.13 = (f32[1,1,64,32]{3,2,1,0:T(8,128)S(1)}, f32[1,1,64,32]{3,2,1,0:T(8,128)}, u32[]{:S(2)}) copy-start(f32[1,1,64,32]{3,2,1,0:T(8,128)} %copy-done.12) | copy-start | bytes 24580
  34.5 281.8 %copy-start.14 = (f32[2048]{0:T(1024)S(1)}, f32[2048]{0:T(1024)}, u32[]{:S(2)}) copy-start(f32[2048]{0:T(1024)} %mul.268) | copy-start | bytes 24580
  34.5 281.8 %copy-start.15 = (f32[1,1,64]{2,1,0:T(1,128)S(1)}, f32[1,1,64]{2,1,0:T(1,128)}, u32[]{:S(2)}) copy-start(f32[1,1,64]{2,1,0:T(1,128)} %get-tuple-element.961) | copy-start | bytes 772
  34.5 281.8 %copy-start.16 = (f32[1,1,64]{2,1,0:T(1,128)S(1)}, f32[1,1,64]{2,1,0:T(1,128)}, u32[]{:S(2)}) copy-start(f32[1,1,64]{2,1,0:T(1,128)} %get-tuple-element.959) | copy-start | bytes 772
  38.0 3.2 copy-start
  98.6 3.8 copy-start.2
  107.9 3.2 copy-start
  168.5 3.8 copy-start.2
  177.8 3.2 copy-start
  238.4 3.8 copy-start.2
  247.7 3.2 copy-start
  308.3 3.8 copy-start.2
  381.6 3.8 copy-start.3
  452.5 3.8 copy-start.3
  523.3 3.8 copy-start.3
  594.2 3.8 copy-start.3
  602.6 3.8 copy-start.6
  602.6 6.7 %copy-start.11 = (f32[64,32]{1,0:T(8,128)S(1)}, f32[64,32]{1,0:T(8,128)}, u32[]{:S(2)}) copy-start(f32[64,32]{1,0:T(8,128)} %copy-done.10) | copy-start | bytes 24580
  602.6 6.8 %copy-start.5 = (f32[2048,128]{1,0:T(8,128)S(1)}, f32[2048,128]{1,0:T(8,128)}, u32[]{:S(2)}) copy-start(f32[2048,128]{1,0:T(8,128)} %copy-done.4) | copy-start | bytes 3145732
  607.3 15.6 %collective-permute-start.1 = (bf16[3072,128]{1,0:T(8,128)(2,1)}, bf16[3072,128]{1,0:T(8,128)(2,1)}, u32[]{:S(2)}, u32[]{:S(2)}) collective-permute-start(bf16[3072,128]{1,0:T(8,128)(2,1)} %slice.88), channel_id=1, source_target_pairs={{1,0},{2,1},{3,2},{4,3},{5,4},{6,5},{7,6},{8,7},{9,8},{10,9},{11,1... | collective-permute-start | bytes 2359304 | tf_op jit(solution)/shard_map/ppermute | solution.py:15
  (9 other events, 20.3 us)
where the time goes:
time: 635 us; the launch traced here: 626 us
  local copies, waits for them, and re-layouts  339 us (53%)
  other arithmetic  193 us (30%)
  matrix products  64 us (10%)
  waiting for transfers between devices  16.2 us (3%)
  between operations  7.39 us (1%)
    mul x16, local copies, waits for them, and re-layouts, block_terms(): delta[:, None, :] * weight_rows[:, :, None] * factor  108 us
    mul x16, local copies, waits for them, and re-layouts, block_terms(): weight_part = jnp.sum(delta[:, None, :] * active, axis=2)  107 us
    reduce_sum x8, other arithmetic, block_terms(): weight_part = jnp.sum(delta[:, None, :] * active, axis=2)  96 us
    max x8, local copies, waits for them, and re-layouts, block_terms(): active = jnp.maximum(scores, 0.0) * factor  74.4 us
    reduce_sum x8, other arithmetic, block_terms(): index_value = jnp.sum(weight_rows[:, :, None] * active, axis=1)  38.3 us
    max x8, other arithmetic, block_terms(): active = jnp.maximum(scores, 0.0) * factor  32.8 us
    dot_general x8, matrix products, block_terms(): jnp.dot(score_grad, key_block, preferred_element_type=jnp.float32)  29.9 us
    while x32, local copies, waits for them, and re-layouts  25.9 us
  transfers between devices with their start and end apart: 2, of which 2 were waited for; matrix products, arithmetic and copies ran while one was open for 2% of the time, Pallas kernels for 0%

commit v1 on v0

v1 whole, which is shorter than its diff:
```python
import jax
import jax.numpy as jnp
from jax import lax
from jax.experimental import pallas as pl
from jax.experimental.pallas import tpu as pltpu
from jax.sharding import PartitionSpec as P

BLK = 1024
QT = 64
H = 32
DH = 128
KB_DEV = 8
TASKS = 2
RIM = 3
SLOTS = 4
NT = 256
FACTOR = 1.0 / DH**0.5
MESH = pl.DeviceIdType.MESH
F32 = jnp.float32
BF16 = jnp.bfloat16


def lanes2(x):
    return jnp.concatenate([x, x], axis=1)


def kernel(
    slot_ref, doc_ref, w_ref, norm_ref, cot_ref, q_hbm, t_hbm, k_hbm,
    qg_hbm, wg_ref, kg_hbm,
    k_v, t_v, q_raw, q_h, qw_t, w_b, n_b, c_b, s_v, u_v, dk_v,
    rim_v, lend_v, lent_v, qg_v, kg_v,
    in_sem, rim_send, rim_recv, lend_send, lend_recv, out_sem,
):
    me = lax.axis_index("ctx")
    size = lax.axis_size("ctx")
    nxt = lax.rem(me + 1, size)
    prv = lax.rem(me + size - 1, size)
    base = me * (KB_DEV * BLK)

    load_q = pltpu.make_async_copy(q_hbm.at[0], q_raw, in_sem.at[0])
    loads = [
        pltpu.make_async_copy(
            k_hbm.at[0, pl.ds(b * BLK, BLK), :], k_v.at[RIM + b], in_sem.at[1 + b]
        )
        for b in range(KB_DEV)
    ]
    loads += [
        pltpu.make_async_copy(
            t_hbm.at[0, i, :, pl.ds(j * BLK, BLK)],
            t_v.at[i, j],
            in_sem.at[1 + KB_DEV + i * SLOTS + j],
        )
        for i in range(TASKS)
        for j in range(SLOTS)
    ]
    load_q.start()
    for load in loads:
        load.start()

    barrier = pltpu.get_barrier_semaphore()
    for other in (prv, nxt):
        pl.semaphore_signal(barrier, inc=1, device_id={"ctx": other}, device_id_type=MESH)
    pl.semaphore_wait(barrier, 2)

    def rim_copy(r):
        return pltpu.make_async_remote_copy(
            src_ref=k_hbm.at[0, pl.ds((KB_DEV - RIM + r) * BLK, BLK), :],
            dst_ref=rim_v.at[r],
            send_sem=rim_send.at[r],
            recv_sem=rim_recv.at[r],
            device_id={"ctx": nxt},
            device_id_type=MESH,
        )

    def lend_copy(r):
        return pltpu.make_async_remote_copy(
            src_ref=lend_v.at[r],
            dst_ref=lent_v.at[r],
            send_sem=lend_send.at[r],
            recv_sem=lend_recv.at[r],
            device_id={"ctx": prv},
            device_id_type=MESH,
        )

    for r in range(RIM):
        rim_copy(r).start()

    load_q.wait()
    for i in range(TASKS):
        w_all = w_ref[0, i] * FACTOR
        n_b[i] = jnp.broadcast_to(norm_ref[0, i : i + 1, :], (128, QT)).T
        c_b[i] = jnp.broadcast_to(cot_ref[0, i : i + 1, :], (128, QT)).T
        for pair in range(H // 2):
            parts = []
            for h in (2 * pair, 2 * pair + 1):
                wide = jnp.broadcast_to(w_all[:, h : h + 1], (QT, DH))
                rows = q_raw[i, :, h * DH : (h + 1) * DH]
                w_b[i, h * QT : (h + 1) * QT, :] = wide
                q_h[i, h * QT : (h + 1) * QT, :] = rows
                parts.append(rows.astype(F32) * wide)
            both = jnp.concatenate(parts, axis=0).astype(BF16)
            qw_t[i, :, pair * 128 : (pair + 1) * 128] = both.T

    def place(i, p):
        last = slot_ref[0, i] // (BLK // QT)
        if p is None:
            return last
        r = p - 1
        return last - 1 - lax.rem(last + 2 - r, 3)

    def process(i, p):
        diag = p is None
        block = place(i, p)
        query_first = slot_ref[0, i] * QT
        doc = doc_ref[0, i] - base
        first = (doc + SLOTS * BLK) // BLK - SLOTS
        column = jnp.clip(block - first, 0, SLOTS - 1)
        keys = k_v[RIM + block]
        keys_t = keys.T
        norm = lanes2(n_b[i])
        cot = lanes2(c_b[i])
        q_pos = lax.broadcasted_iota(jnp.int32, (QT, NT), 0) + query_first
        lane = lax.broadcasted_iota(jnp.int32, (QT, NT), 1)
        for n in range(BLK // NT):
            cols = slice(n * NT, (n + 1) * NT)
            index = jnp.zeros((QT, NT), F32)
            for pair in range(H // 2):
                s = jnp.dot(
                    q_h[i, pair * 128 : (pair + 1) * 128, :],
                    keys_t[:, cols],
                    preferred_element_type=F32,
                )
                s_v[pair * 128 : (pair + 1) * 128, cols] = s.astype(BF16)
                for e in range(2):
                    h = 2 * pair + e
                    w = lanes2(w_b[i, h * QT : (h + 1) * QT, :])
                    index += jnp.maximum(s[e * QT : (e + 1) * QT], 0.0) * w
            target = t_v[i, column, :, cols].astype(F32)
            k_pos = lane + (block * BLK + n * NT)
            live = (k_pos >= doc) & (k_pos <= q_pos)
            delta = jnp.where(live, cot * (jnp.exp(index - norm) - target), 0.0).astype(BF16)
            zero = jnp.zeros_like(delta)
            for h in range(H):
                rows = slice(h * QT, (h + 1) * QT)
                s_v[rows, cols] = jnp.where(s_v[rows, cols] > 0, delta, zero)
        u = jnp.dot(s_v[...], keys, preferred_element_type=F32)
        if diag:
            u_v[i] = u
        else:
            u_v[i] += u
        d_t = jnp.dot(qw_t[i], s_v[...], preferred_element_type=F32)
        dk_v[i, 0 if diag else p] = d_t.T

    for i in range(TASKS):
        dk_v[i, SLOTS] = jnp.zeros((BLK, DH), F32)
    for load in loads:
        load.wait()

    @pl.loop(0, TASKS)
    def _(i):
        process(i, None)

    @pl.loop(1, SLOTS)
    def _(p):
        rim_copy(p - 1).wait_recv()
        k_v[p - 1] = rim_v[p - 1]

        @pl.loop(0, TASKS)
        def _(i):
            process(i, p)

        total = jnp.zeros((BLK, DH), F32)
        for i in range(TASKS):
            total += dk_v[i, jnp.where(place(i, p) < 0, p, SLOTS)]
        lend_v[p - 1] = total.astype(BF16)
        lend_copy(p - 1).start()

    def own(b):
        total = jnp.zeros((BLK, DH), F32)
        for i in range(TASKS):
            last = place(i, None)
            inside = (b <= last) & (b >= last - RIM)
            p = jnp.where(last == b, 0, 1 + b % 3)
            total += dk_v[i, jnp.where(inside, p, SLOTS)]
        return total

    def key_out(lo, count, s):
        return pltpu.make_async_copy(
            kg_v.at[pl.ds(lo * BLK, count * BLK), :],
            kg_hbm.at[0, pl.ds(lo * BLK, count * BLK), :],
            out_sem.at[s],
        )

    for b in range(KB_DEV - RIM):
        kg_v[b * BLK : (b + 1) * BLK, :] = own(b).astype(BF16)
    key_out(0, KB_DEV - RIM, 0).start()

    for i in range(TASKS):
        sums = jnp.zeros((QT, 128), F32)
        lane = lax.broadcasted_iota(jnp.int32, (QT, 128), 1)
        for h in range(H):
            rows = slice(h * QT, (h + 1) * QT)
            u = u_v[i, rows, :]
            qg_v[i, :, h * DH : (h + 1) * DH] = (u * w_b[i, rows, :]).astype(BF16)
            dots = jnp.sum(u * q_h[i, rows, :].astype(F32), axis=1, keepdims=True)
            sums = jnp.where(lane == h, dots, sums)
        wg_ref[0, i] = sums[:, :H] * FACTOR
    query_out = pltpu.make_async_copy(qg_v, qg_hbm.at[0], out_sem.at[1])
    query_out.start()

    for r in range(RIM):
        lend_copy(r).wait_recv()
        b = KB_DEV - RIM + r
        kg_v[b * BLK : (b + 1) * BLK, :] = (own(b) + lent_v[r].astype(F32)).astype(BF16)
    key_out(KB_DEV - RIM, RIM, 2).start()

    for r in range(RIM):
        rim_copy(r).wait_send()
        lend_copy(r).wait_send()
    key_out(0, KB_DEV - RIM, 0).wait()
    query_out.wait()
    key_out(KB_DEV - RIM, RIM, 2).wait()


def local(queries, head_weights, key_vectors, targets, normalizers, loss_grad, tile_slot, doc_start):
    rows = H * QT
    vmem = pl.BlockSpec(memory_space=pltpu.VMEM)
    smem = pl.BlockSpec(memory_space=pltpu.SMEM)
    hbm = pl.BlockSpec(memory_space=pl.ANY)
    dma = pltpu.SemaphoreType.DMA
    return pl.pallas_call(
        kernel,
        out_shape=(
            jax.ShapeDtypeStruct(queries.shape, BF16),
            jax.ShapeDtypeStruct(head_weights.shape, F32),
            jax.ShapeDtypeStruct(key_vectors.shape, BF16),
        ),
        in_specs=[smem, smem, vmem, vmem, vmem, hbm, hbm, hbm],
        out_specs=(hbm, vmem, hbm),
        scratch_shapes=[
            pltpu.VMEM((RIM + KB_DEV, BLK, DH), BF16),
            pltpu.VMEM((TASKS, SLOTS, QT, BLK), BF16),
            pltpu.VMEM((TASKS, QT, H * DH), BF16),
            pltpu.VMEM((TASKS, rows, DH), BF16),
            pltpu.VMEM((TASKS, DH, rows), BF16),
            pltpu.VMEM((TASKS, rows, DH), F32),
            pltpu.VMEM((TASKS, QT, 128), F32),
            pltpu.VMEM((TASKS, QT, 128), F32),
            pltpu.VMEM((rows, BLK), BF16),
            pltpu.VMEM((TASKS, rows, DH), F32),
            pltpu.VMEM((TASKS, SLOTS + 1, BLK, DH), F32),
            pltpu.VMEM((RIM, BLK, DH), BF16),
            pltpu.VMEM((RIM, BLK, DH), BF16),
            pltpu.VMEM((RIM, BLK, DH), BF16),
            pltpu.VMEM((TASKS, QT, H * DH), BF16),
            pltpu.VMEM((KB_DEV * BLK, DH), BF16),
            dma((1 + KB_DEV + TASKS * SLOTS,)),
            dma((RIM,)),
            dma((RIM,)),
            dma((RIM,)),
            dma((RIM,)),
            dma((3,)),
        ],
        compiler_params=pltpu.CompilerParams(
            collective_id=0, has_side_effects=True, vmem_limit_bytes=60 << 20
        ),
    )(tile_slot, doc_start, head_weights, normalizers, loss_grad, queries, targets, key_vectors)


def solution(mesh):
    return jax.shard_map(
        local,
        mesh=mesh,
        in_specs=(
            P("sec", "ctx", None, None),
            P("sec", "ctx", None, None),
            P("sec", "ctx", None),
            P("sec", "ctx", None, None),
            P("sec", "ctx", None),
            P("sec", "ctx", None),
            P("sec", "ctx"),
            P("sec", "ctx"),
        ),
        out_specs=(P("sec", "ctx", None, None), P("sec", "ctx", None, None), P("sec", "ctx", None)),
        check_vma=False,
    )
```

time: 635 us -> 59.1 us (0.09)
  the two profiles are of different devices: /device:TPU:24 before, /device:TPU:1 now
where the time goes in v1:
time: 59.1 us; the launch traced here: 58.9 us
  Pallas kernels  51.5 us (87%)
  local copies, waits for them, and re-layouts  6.76 us (11%)
  between operations  0.65 us (1%)
    pallas_call x1, Pallas kernels, local(): pl.pallas_call(kernel, out_shape=(jax.ShapeDtypeStruct(queries.shape, BF1...  51.5 us
    unnamed x5, local copies, waits for them, and re-layouts  5.08 us
    pallas_call x1, local copies, waits for them, and re-layouts, local(): pl.pallas_call(kernel, out_shape=(jax.ShapeDtypeStruct(queries.shape, BF1...  1.68 us

profile of v1, /device:TPU:1, one launch (start us, length us, event | category | flops | bytes accessed | tf_op | source)
XLA Modules:
  0.0 58.9 jit_solution(8548720438079426841)
XLA Ops:
  0.6 1.5 %copy.11.w_ref = f32[1,2,64,32]{3,2,1,0:T(8,128)} copy(f32[1,2,64,32]{2,3,1,0:T(8,128)} %param.9) | data formatting | bytes 32768 | tf_op args[1]
  2.1 51.5 %shard_map.103 = (bf16[1,2,64,4096]{3,2,1,0:T(8,128)(2,1)}, f32[1,2,64,32]{3,2,1,0:T(8,128)}, bf16[1,8192,128]{2,1,0:T(8,128)(2,1)}) custom-call(s32[1,2]{1,0:T(1,128)} %slot_ref.1, s32[1,2]{1,0:T(1,128)} %doc_ref.1, f32[1,2,64,32]{3,2,1,0:T(8,128)} %copy.11.w_ref, f32[1,2,64]{2,1,0:T(2,128)} %norm_ref.1, f32[1,2,64]{2,1,0:T(2,128)} %cot_ref.1, ...), custom_call_target="tpu_custom_call" | custom-call | tf_op jit(solution)/shard_map/pallas_call | solution.py:231
  53.6 0.0 copy-start
  53.6 1.7 %copy.12 = f32[1,2,64,32]{2,3,1,0:T(8,128)} copy(f32[1,2,64,32]{3,2,1,0:T(8,128)} %get-tuple-element.4) | data formatting | bytes 32768 | tf_op jit(solution)/shard_map/pallas_call | solution.py:231
  55.3 2.3 %copy.15 = bf16[1,2,64,4096]{3,2,1,0:T(8,128)(2,1)} copy(bf16[1,2,64,4096]{3,2,1,0:T(8,128)(2,1)} %get-tuple-element.9) | data formatting | bytes 2097152
  57.5 0.0 copy-done
  57.5 1.3 %copy.16 = bf16[1,8192,128]{2,1,0:T(8,128)(2,1)} copy(bf16[1,8192,128]{2,1,0:T(8,128)(2,1)S(1)} %copy-done) | data formatting | bytes 4194304
Async XLA Ops:
  53.6 4.0 %copy-start = (bf16[1,8192,128]{2,1,0:T(8,128)(2,1)S(1)}, bf16[1,8192,128]{2,1,0:T(8,128)(2,1)}, u32[]{:S(2)}) copy-start(bf16[1,8192,128]{2,1,0:T(8,128)(2,1)} %get-tuple-element.11) | copy-start | bytes 6291460

commit v2 on v1

v2 whole, which is shorter than its diff:
```python
import jax
import jax.numpy as jnp
from jax import lax
from jax.experimental import pallas as pl
from jax.experimental.pallas import tpu as pltpu
from jax.sharding import PartitionSpec as P

BLK = 1024
QT = 64
H = 32
DH = 128
KB_DEV = 8
TASKS = 2
RIM = 3
SLOTS = 4
NT = 256
FACTOR = 1.0 / DH**0.5
MESH = pl.DeviceIdType.MESH
F32 = jnp.float32
BF16 = jnp.bfloat16


def lanes2(x):
    return jnp.concatenate([x, x], axis=1)


def kernel(
    slot_ref, doc_ref, w_ref, norm_ref, cot_ref, q_hbm, t_hbm, k_hbm,
    qg_v, wg_ref, kg_v,
    k_v, t_v, q_raw, q_h, qw_t, w_b, n_b, c_b, s_v, u_v, dk_v,
    rim_v, lend_v, lent_v,
    in_sem, rim_send, rim_recv, lend_send, lend_recv,
):
    me = lax.axis_index("ctx")
    size = lax.axis_size("ctx")
    nxt = lax.rem(me + 1, size)
    prv = lax.rem(me + size - 1, size)
    base = me * (KB_DEV * BLK)

    load_q = pltpu.make_async_copy(q_hbm.at[0], q_raw, in_sem.at[0])
    loads = [
        pltpu.make_async_copy(
            k_hbm.at[0, pl.ds(b * BLK, BLK), :], k_v.at[RIM + b], in_sem.at[1 + b]
        )
        for b in range(KB_DEV)
    ]
    loads += [
        pltpu.make_async_copy(
            t_hbm.at[0, i, :, pl.ds(j * BLK, BLK)],
            t_v.at[i, j],
            in_sem.at[1 + KB_DEV + i * SLOTS + j],
        )
        for i in range(TASKS)
        for j in range(SLOTS)
    ]
    load_q.start()
    for load in loads:
        load.start()

    barrier = pltpu.get_barrier_semaphore()
    for other in (prv, nxt):
        pl.semaphore_signal(barrier, inc=1, device_id={"ctx": other}, device_id_type=MESH)
    pl.semaphore_wait(barrier, 2)

    def rim_copy(r):
        return pltpu.make_async_remote_copy(
            src_ref=k_hbm.at[0, pl.ds((KB_DEV - RIM + r) * BLK, BLK), :],
            dst_ref=rim_v.at[r],
            send_sem=rim_send.at[r],
            recv_sem=rim_recv.at[r],
            device_id={"ctx": nxt},
            device_id_type=MESH,
        )

    def lend_copy(r):
        return pltpu.make_async_remote_copy(
            src_ref=lend_v.at[r],
            dst_ref=lent_v.at[r],
            send_sem=lend_send.at[r],
            recv_sem=lend_recv.at[r],
            device_id={"ctx": prv},
            device_id_type=MESH,
        )

    for r in range(RIM):
        rim_copy(r).start()

    load_q.wait()
    for i in range(TASKS):
        w_all = w_ref[0, i].T * FACTOR
        n_b[i][...] = jnp.broadcast_to(norm_ref[0, i : i + 1, :], (128, QT)).T
        c_b[i][...] = jnp.broadcast_to(cot_ref[0, i : i + 1, :], (128, QT)).T
        for pair in range(H // 2):
            parts = []
            for h in (2 * pair, 2 * pair + 1):
                wide = jnp.broadcast_to(w_all[:, h : h + 1], (QT, DH))
                rows = q_raw[i, :, h * DH : (h + 1) * DH]
                w_b[i][h * QT : (h + 1) * QT, :] = wide
                q_h[i][h * QT : (h + 1) * QT, :] = rows
                parts.append(rows.astype(F32) * wide)
            both = jnp.concatenate(parts, axis=0).astype(BF16)
            qw_t[i][:, pair * 128 : (pair + 1) * 128] = both.T

    def place(i, p):
        last = slot_ref[0, i] // (BLK // QT)
        return jnp.where(p == 0, last, last - 1 - lax.rem(last + 3 - p, 3))

    def process(i, p):
        block = place(i, p)
        query_first = slot_ref[0, i] * QT
        doc = doc_ref[0, i] - base
        first = (doc + SLOTS * BLK) // BLK - SLOTS
        column = jnp.clip(block - first, 0, SLOTS - 1)
        keys = k_v[RIM + block]
        keys_t = keys.T
        norm = lanes2(n_b[i][...])
        cot = lanes2(c_b[i][...])
        q_pos = lax.broadcasted_iota(jnp.int32, (QT, NT), 0) + query_first
        lane = lax.broadcasted_iota(jnp.int32, (QT, NT), 1)
        for n in range(BLK // NT):
            cols = slice(n * NT, (n + 1) * NT)
            index = jnp.zeros((QT, NT), F32)
            for pair in range(H // 2):
                s = jnp.dot(
                    q_h[i][pair * 128 : (pair + 1) * 128, :],
                    keys_t[:, cols],
                    preferred_element_type=F32,
                )
                s_v[pair * 128 : (pair + 1) * 128, cols] = s.astype(BF16)
                for e in range(2):
                    h = 2 * pair + e
                    w = lanes2(w_b[i][h * QT : (h + 1) * QT, :])
                    index += jnp.maximum(s[e * QT : (e + 1) * QT], 0.0) * w
            target = t_v[i, column, :, cols].astype(F32)
            k_pos = lane + (block * BLK + n * NT)
            live = (k_pos >= doc) & (k_pos <= q_pos)
            delta = jnp.where(live, cot * (jnp.exp(index - norm) - target), 0.0).astype(BF16)
            zero = jnp.zeros_like(delta)
            for h in range(H):
                rows = slice(h * QT, (h + 1) * QT)
                s_v[rows, cols] = jnp.where(s_v[rows, cols] > 0, delta, zero)
        u = jnp.dot(s_v[...], keys, preferred_element_type=F32)
        u_v[i][...] += u
        d_t = jnp.dot(qw_t[i][...], s_v[...], preferred_element_type=F32)
        dk_v[i][p] = d_t.T

    for i in range(TASKS):
        dk_v[i][SLOTS] = jnp.zeros((BLK, DH), F32)
        u_v[i][...] = jnp.zeros((H * QT, DH), F32)
    for load in loads:
        load.wait()

    @pl.loop(0, SLOTS)
    def _(p):
        @pl.when(p > 0)
        def _():
            rim_copy(p - 1).wait_recv()
            k_v[p - 1] = rim_v[p - 1]

        for i in range(TASKS):
            process(i, p)

        @pl.when(p > 0)
        def _():
            total = jnp.zeros((BLK, DH), F32)
            for i in range(TASKS):
                total += dk_v[i][jnp.where(place(i, p) < 0, p, SLOTS)]
            lend_v[p - 1] = total.astype(BF16)
            lend_copy(p - 1).start()

    def own(b):
        total = jnp.zeros((BLK, DH), F32)
        for i in range(TASKS):
            last = slot_ref[0, i] // (BLK // QT)
            inside = (b <= last) & (b >= last - RIM)
            p = jnp.where(last == b, 0, 1 + b % 3)
            total += dk_v[i][jnp.where(inside, p, SLOTS)]
        return total

    for b in range(KB_DEV - RIM):
        kg_v[0, b * BLK : (b + 1) * BLK, :] = own(b).astype(BF16)

    for i in range(TASKS):
        sums = jnp.zeros((QT, 128), F32)
        lane = lax.broadcasted_iota(jnp.int32, (QT, 128), 1)
        for h in range(H):
            rows = slice(h * QT, (h + 1) * QT)
            u = u_v[i][rows, :]
            qg_v[0, i, :, h * DH : (h + 1) * DH] = (u * w_b[i][rows, :]).astype(BF16)
            dots = jnp.sum(u * q_h[i][rows, :].astype(F32), axis=1, keepdims=True)
            sums = jnp.where(lane == h, dots, sums)
        wg_ref[0, i] = (sums * FACTOR).T[:H, :]

    for r in range(RIM):
        lend_copy(r).wait_recv()
        b = KB_DEV - RIM + r
        kg_v[0, b * BLK : (b + 1) * BLK, :] = (own(b) + lent_v[r].astype(F32)).astype(BF16)

    for r in range(RIM):
        rim_copy(r).wait_send()
        lend_copy(r).wait_send()


def write_out(*refs):
    copies = [
        pltpu.make_async_copy(refs[j], refs[3 + j], refs[6].at[j]) for j in range(3)
    ]
    for copy in copies:
        copy.start()
    for copy in copies:
        copy.wait()


def local(queries, head_weights, key_vectors, targets, normalizers, loss_grad, tile_slot, doc_start):
    rows = H * QT
    vmem = pl.BlockSpec(memory_space=pltpu.VMEM)
    smem = pl.BlockSpec(memory_space=pltpu.SMEM)
    hbm = pl.BlockSpec(memory_space=pltpu.HBM)
    dma = pltpu.SemaphoreType.DMA
    grads = pl.pallas_call(
        kernel,
        out_shape=(
            pltpu.VMEM(queries.shape, BF16),
            pltpu.VMEM((1, TASKS, H, QT), F32),
            pltpu.VMEM(key_vectors.shape, BF16),
        ),
        in_specs=[smem, smem, vmem, vmem, vmem, hbm, hbm, hbm],
        out_specs=(vmem, vmem, vmem),
        scratch_shapes=[
            pltpu.VMEM((RIM + KB_DEV, BLK, DH), BF16),
            pltpu.VMEM((TASKS, SLOTS, QT, BLK), BF16),
            pltpu.VMEM((TASKS, QT, H * DH), BF16),
            [pltpu.VMEM((rows, DH), BF16)] * TASKS,
            [pltpu.VMEM((DH, rows), BF16)] * TASKS,
            [pltpu.VMEM((rows, DH), F32)] * TASKS,
            [pltpu.VMEM((QT, 128), F32)] * TASKS,
            [pltpu.VMEM((QT, 128), F32)] * TASKS,
            pltpu.VMEM((rows, BLK), BF16),
            [pltpu.VMEM((rows, DH), F32)] * TASKS,
            [pltpu.VMEM((SLOTS + 1, BLK, DH), F32)] * TASKS,
            pltpu.VMEM((RIM, BLK, DH), BF16),
            pltpu.VMEM((RIM, BLK, DH), BF16),
            pltpu.VMEM((RIM, BLK, DH), BF16),
            dma((1 + KB_DEV + TASKS * SLOTS,)),
            dma((RIM,)),
            dma((RIM,)),
            dma((RIM,)),
            dma((RIM,)),
        ],
        compiler_params=pltpu.CompilerParams(
            collective_id=0, has_side_effects=True, vmem_limit_bytes=56 << 20
        ),
    )(
        tile_slot, doc_start, jnp.swapaxes(head_weights, 2, 3), normalizers, loss_grad,
        queries, targets, key_vectors,
    )
    query_grad, weight_grad, key_grad = pl.pallas_call(
        write_out,
        out_shape=[jax.ShapeDtypeStruct(g.shape, g.dtype) for g in grads],
        in_specs=[vmem] * 3,
        out_specs=[hbm] * 3,
        scratch_shapes=[dma((3,))],
        compiler_params=pltpu.CompilerParams(vmem_limit_bytes=1 << 20),
    )(*[pltpu.with_memory_space_constraint(g, pltpu.VMEM) for g in grads])
    return query_grad, jnp.swapaxes(weight_grad, 2, 3), key_grad


def solution(mesh):
    return jax.shard_map(
        local,
        mesh=mesh,
        in_specs=(
            P("sec", "ctx", None, None),
            P("sec", "ctx", None, None),
            P("sec", "ctx", None),
            P("sec", "ctx", None, None),
            P("sec", "ctx", None),
            P("sec", "ctx", None),
            P("sec", "ctx"),
            P("sec", "ctx"),
        ),
        out_specs=(P("sec", "ctx", None, None), P("sec", "ctx", None, None), P("sec", "ctx", None)),
        check_vma=False,
    )
```

time: 59.1 us -> 44.9 us (0.76)
  the two profiles are of different devices: /device:TPU:1 before, /device:TPU:4 now
where the time goes in v2:
time: 44.9 us; the launch traced here: 44.7 us
  Pallas kernels  44.1 us (98%)
  between operations  0.64 us (1%)
    pallas_call x1, Pallas kernels, local(): pl.pallas_call(kernel, out_shape=(pltpu.VMEM(queries.shape, BF16), pltpu....  42.4 us
    pallas_call x1, Pallas kernels, local(): pl.pallas_call(write_out, out_shape=[jax.ShapeDtypeStruct(g.shape, g.dtyp...  1.7 us

profile of v2, /device:TPU:4, one launch (start us, length us, event | category | flops | bytes accessed | tf_op | source)
XLA Modules:
  0.0 44.7 jit_solution(18342447762159501301)
XLA Ops:
  0.6 42.4 %shard_map.103 = (bf16[1,2,64,4096]{3,2,1,0:T(8,128)(2,1)S(1)}, f32[1,2,32,64]{3,2,1,0:T(8,128)S(1)}, bf16[1,8192,128]{2,1,0:T(8,128)(2,1)S(1)}) custom-call(s32[1,2]{1,0:T(1,128)} %slot_ref.1, s32[1,2]{1,0:T(1,128)} %doc_ref.1, f32[1,2,32,64]{3,2,1,0:T(8,128)} %bitcast.2, f32[1,2,64]{2,1,0:T(2,128)} %norm_ref.1, f32[1,2,64]{2,1,0:T(2,128)} %cot_ref.1, ...), custom_call_target="tpu_custom_call" | custom-call | tf_op jit(solution)/shard_map/pallas_call | solution.py:220
  43.0 1.7 %shard_map.104 = (bf16[1,2,64,4096]{3,2,1,0:T(8,128)(2,1)}, f32[1,2,32,64]{3,2,1,0:T(8,128)}, bf16[1,8192,128]{2,1,0:T(8,128)(2,1)}) custom-call(bf16[1,2,64,4096]{3,2,1,0:T(8,128)(2,1)S(1)} %get-tuple-element.9.refs_0_, f32[1,2,32,64]{3,2,1,0:T(8,128)S(1)} %get-tuple-element.10.refs_1_, bf16[1,8192,128]{2,1,0:T(8,128)(2,1)S(1)} %get-tuple-element.11.refs_2_), custom_call_target="tpu_custom_call" | custom-call | tf_op jit(solution)/shard_map/pallas_call | solution.py:257

commit v3 on v2

--- a/solution.py
+++ b/solution.py
@@ -14,6 +14,9 @@
 RIM = 3
 SLOTS = 4
 NT = 256
+CUT = 2
+PART = BLK // CUT
+LENT = RIM * CUT
 FACTOR = 1.0 / DH**0.5
 MESH = pl.DeviceIdType.MESH
 F32 = jnp.float32
@@ -33,38 +36,35 @@
 ):
     me = lax.axis_index("ctx")
     size = lax.axis_size("ctx")
-    nxt = lax.rem(me + 1, size)
-    prv = lax.rem(me + size - 1, size)
+    nxt = jnp.minimum(me + 1, size - 1)
+    prv = jnp.maximum(me - 1, 0)
+    has_prev = me > 0
+    has_next = me < size - 1
     base = me * (KB_DEV * BLK)
 
     load_q = pltpu.make_async_copy(q_hbm.at[0], q_raw, in_sem.at[0])
     loads = [
         pltpu.make_async_copy(
-            k_hbm.at[0, pl.ds(b * BLK, BLK), :], k_v.at[RIM + b], in_sem.at[1 + b]
+            k_hbm.at[0, pl.ds(b * PART, PART), :], k_v.at[LENT + b], in_sem.at[1 + b]
         )
-        for b in range(KB_DEV)
+        for b in range(KB_DEV * CUT)
     ]
     loads += [
         pltpu.make_async_copy(
-            t_hbm.at[0, i, :, pl.ds(j * BLK, BLK)],
+            t_hbm.at[0, i, :, pl.ds(j * PART, PART)],
             t_v.at[i, j],
-            in_sem.at[1 + KB_DEV + i * SLOTS + j],
+            in_sem.at[1 + CUT * (KB_DEV + i * SLOTS) + j],
         )
         for i in range(TASKS)
-        for j in range(SLOTS)
+        for j in range(SLOTS * CUT)
     ]
     load_q.start()
     for load in loads:
         load.start()
 
-    barrier = pltpu.get_barrier_semaphore()
-    for other in (prv, nxt):
-        pl.semaphore_signal(barrier, inc=1, device_id={"ctx": other}, device_id_type=MESH)
-    pl.semaphore_wait(barrier, 2)
-
     def rim_copy(r):
         return pltpu.make_async_remote_copy(
-            src_ref=k_hbm.at[0, pl.ds((KB_DEV - RIM + r) * BLK, BLK), :],
+            src_ref=k_hbm.at[0, pl.ds((KB_DEV * CUT - LENT + r) * PART, PART), :],
             dst_ref=rim_v.at[r],
             send_sem=rim_send.at[r],
             recv_sem=rim_recv.at[r],
@@ -82,11 +82,7 @@
             device_id_type=MESH,
         )
 
-    for r in range(RIM):
-        rim_copy(r).start()
-
-    load_q.wait()
-    for i in range(TASKS):
+    def prepare(i):
         w_all = w_ref[0, i].T * FACTOR
         n_b[i][...] = jnp.broadcast_to(norm_ref[0, i : i + 1, :], (128, QT)).T
         c_b[i][...] = jnp.broadcast_to(cot_ref[0, i : i + 1, :], (128, QT)).T
@@ -100,24 +96,46 @@
                 parts.append(rows.astype(F32) * wide)
             both = jnp.concatenate(parts, axis=0).astype(BF16)
             qw_t[i][:, pair * 128 : (pair + 1) * 128] = both.T
+        dk_v[i][SLOTS * CUT] = jnp.zeros((PART, DH), F32)
+        u_v[i][...] = jnp.zeros((H * QT, DH), F32)
+
+    barrier = pltpu.get_barrier_semaphore()
+
+    @pl.when(has_prev)
+    def _():
+        pl.semaphore_signal(barrier, inc=1, device_id={"ctx": prv}, device_id_type=MESH)
+
+    @pl.when(has_next)
+    def _():
+        pl.semaphore_signal(barrier, inc=1, device_id={"ctx": nxt}, device_id_type=MESH)
+
+    pl.semaphore_wait(barrier, has_prev.astype(jnp.int32) + has_next.astype(jnp.int32))
+
+    @pl.when(has_next)
+    def _():
+        for r in range(LENT):
+            rim_copy(r).start()
+
+    load_q.wait()
+    for i in range(TASKS):
+        prepare(i)
 
     def place(i, p):
         last = slot_ref[0, i] // (BLK // QT)
         return jnp.where(p == 0, last, last - 1 - lax.rem(last + 3 - p, 3))
 
-    def process(i, p):
+    def mask_times_delta(i, p, c, keys):
         block = place(i, p)
         query_first = slot_ref[0, i] * QT
         doc = doc_ref[0, i] - base
         first = (doc + SLOTS * BLK) // BLK - SLOTS
         column = jnp.clip(block - first, 0, SLOTS - 1)
-        keys = k_v[RIM + block]
         keys_t = keys.T
         norm = lanes2(n_b[i][...])
         cot = lanes2(c_b[i][...])
         q_pos = lax.broadcasted_iota(jnp.int32, (QT, NT), 0) + query_first
         lane = lax.broadcasted_iota(jnp.int32, (QT, NT), 1)
-        for n in range(BLK // NT):
+        for n in range(PART // NT):
             cols = slice(n * NT, (n + 1) * NT)
             index = jnp.zeros((QT, NT), F32)
             for pair in range(H // 2):
@@ -131,54 +149,74 @@
                     h = 2 * pair + e
                     w = lanes2(w_b[i][h * QT : (h + 1) * QT, :])
                     index += jnp.maximum(s[e * QT : (e + 1) * QT], 0.0) * w
-            target = t_v[i, column, :, cols].astype(F32)
-            k_pos = lane + (block * BLK + n * NT)
+            target = t_v[i, column * CUT + c, :, cols].astype(F32)
+            k_pos = lane + (block * BLK + c * PART + n * NT)
             live = (k_pos >= doc) & (k_pos <= q_pos)
             delta = jnp.where(live, cot * (jnp.exp(index - norm) - target), 0.0).astype(BF16)
             zero = jnp.zeros_like(delta)
             for h in range(H):
                 rows = slice(h * QT, (h + 1) * QT)
                 s_v[rows, cols] = jnp.where(s_v[rows, cols] > 0, delta, zero)
-        u = jnp.dot(s_v[...], keys, preferred_element_type=F32)
-        u_v[i][...] += u
+
+    def query_part(i, keys):
+        u_v[i][...] += jnp.dot(s_v[...], keys, preferred_element_type=F32)
+
+    def key_part(i, unit):
         d_t = jnp.dot(qw_t[i][...], s_v[...], preferred_element_type=F32)
-        dk_v[i][p] = d_t.T
-
-    for i in range(TASKS):
-        dk_v[i][SLOTS] = jnp.zeros((BLK, DH), F32)
-        u_v[i][...] = jnp.zeros((H * QT, DH), F32)
+        dk_v[i][unit] = d_t.T
+
+    def lend(unit):
+        p = unit // CUT
+        total = jnp.zeros((PART, DH), F32)
+        for i in range(TASKS):
+            total += dk_v[i][jnp.where(place(i, p) < 0, unit, SLOTS * CUT)]
+        lend_v[unit - CUT] = total.astype(BF16)
+
+    def take_rim(r):
+        @pl.when(has_prev)
+        def _():
+            rim_copy(r).wait_recv()
+            k_v[r] = rim_v[r]
+
+    @pl.when(jnp.logical_not(has_prev))
+    def _():
+        k_v[0:LENT] = jnp.zeros((LENT, PART, DH), BF16)
+
     for load in loads:
         load.wait()
 
-    @pl.loop(0, SLOTS)
-    def _(p):
+    @pl.loop(0, SLOTS * CUT)
+    def _(unit):
+        p = unit // CUT
+        c = unit % CUT
+
         @pl.when(p > 0)
         def _():
-            rim_copy(p - 1).wait_recv()
-            k_v[p - 1] = rim_v[p - 1]
+            take_rim(unit - CUT)
 
         for i in range(TASKS):
-            process(i, p)
-
-        @pl.when(p > 0)
+            keys = k_v[(RIM + place(i, p)) * CUT + c]
+            mask_times_delta(i, p, c, keys)
+            query_part(i, keys)
+            key_part(i, unit)
+
+        @pl.when((p > 0) & has_prev)
         def _():
-            total = jnp.zeros((BLK, DH), F32)
-            for i in range(TASKS):
-                total += dk_v[i][jnp.where(place(i, p) < 0, p, SLOTS)]
-            lend_v[p - 1] = total.astype(BF16)
-            lend_copy(p - 1).start()
-
-    def own(b):
-        total = jnp.zeros((BLK, DH), F32)
+            lend(unit)
+            lend_copy(unit - CUT).start()
+
+    def own(part):
+        b, c = part // CUT, part % CUT
+        total = jnp.zeros((PART, DH), F32)
         for i in range(TASKS):
             last = slot_ref[0, i] // (BLK // QT)
             inside = (b <= last) & (b >= last - RIM)
             p = jnp.where(last == b, 0, 1 + b % 3)
-            total += dk_v[i][jnp.where(inside, p, SLOTS)]
+            total += dk_v[i][jnp.where(inside, p * CUT + c, SLOTS * CUT)]
         return total
 
-    for b in range(KB_DEV - RIM):
-        kg_v[0, b * BLK : (b + 1) * BLK, :] = own(b).astype(BF16)
+    for part in range(KB_DEV * CUT - LENT):
+        kg_v[0, part * PART : (part + 1) * PART, :] = own(part).astype(BF16)
 
     for i in range(TASKS):
         sums = jnp.zeros((QT, 128), F32)
@@ -191,14 +229,29 @@
             sums = jnp.where(lane == h, dots, sums)
         wg_ref[0, i] = (sums * FACTOR).T[:H, :]
 
-    for r in range(RIM):
-        lend_copy(r).wait_recv()
-        b = KB_DEV - RIM + r
-        kg_v[0, b * BLK : (b + 1) * BLK, :] = (own(b) + lent_v[r].astype(F32)).astype(BF16)
-
-    for r in range(RIM):
-        rim_copy(r).wait_send()
-        lend_copy(r).wait_send()
+    @pl.when(has_next)
+    def _():
+        for r in range(LENT):
+            lend_copy(r).wait_recv()
+
+    @pl.when(jnp.logical_not(has_next))
+    def _():
+        lent_v[...] = jnp.zeros((LENT, PART, DH), BF16)
+
+    for r in range(LENT):
+        part = KB_DEV * CUT - LENT + r
+        total = own(part) + lent_v[r].astype(F32)
+        kg_v[0, part * PART : (part + 1) * PART, :] = total.astype(BF16)
+
+    @pl.when(has_next)
+    def _():
+        for r in range(LENT):
+            rim_copy(r).wait_send()
+
+    @pl.when(has_prev)
+    def _():
+        for r in range(LENT):
+            lend_copy(r).wait_send()
 
 
 def write_out(*refs):
@@ -227,25 +280,25 @@
         in_specs=[smem, smem, vmem, vmem, vmem, hbm, hbm, hbm],
         out_specs=(vmem, vmem, vmem),
         scratch_shapes=[
-            pltpu.VMEM((RIM + KB_DEV, BLK, DH), BF16),
-            pltpu.VMEM((TASKS, SLOTS, QT, BLK), BF16),
+            pltpu.VMEM((LENT + KB_DEV * CUT, PART, DH), BF16),
+            pltpu.VMEM((TASKS, SLOTS * CUT, QT, PART), BF16),
             pltpu.VMEM((TASKS, QT, H * DH), BF16),
             [pltpu.VMEM((rows, DH), BF16)] * TASKS,
             [pltpu.VMEM((DH, rows), BF16)] * TASKS,
             [pltpu.VMEM((rows, DH), F32)] * TASKS,
             [pltpu.VMEM((QT, 128), F32)] * TASKS,
             [pltpu.VMEM((QT, 128), F32)] * TASKS,
-            pltpu.VMEM((rows, BLK), BF16),
+            pltpu.VMEM((rows, PART), BF16),
             [pltpu.VMEM((rows, DH), F32)] * TASKS,
-            [pltpu.VMEM((SLOTS + 1, BLK, DH), F32)] * TASKS,
-            pltpu.VMEM((RIM, BLK, DH), BF16),
-            pltpu.VMEM((RIM, BLK, DH), BF16),
-            pltpu.VMEM((RIM, BLK, DH), BF16),
-            dma((1 + KB_DEV + TASKS * SLOTS,)),
-            dma((RIM,)),
-            dma((RIM,)),
-            dma((RIM,)),
-            dma((RIM,)),
+            [pltpu.VMEM((SLOTS * CUT + 1, PART, DH), F32)] * TASKS,
+            pltpu.VMEM((LENT, PART, DH), BF16),
+            pltpu.VMEM((LENT, PART, DH), BF16),
+            pltpu.VMEM((LENT, PART, DH), BF16),
+            dma((1 + CUT * (KB_DEV + TASKS * SLOTS),)),
+            dma((LENT,)),
+            dma((LENT,)),
+            dma((LENT,)),
+            dma((LENT,)),
         ],
         compiler_params=pltpu.CompilerParams(
             collective_id=0, has_side_effects=True, vmem_limit_bytes=56 << 20

time: 44.9 us -> 43.4 us (0.967)
  the two profiles are of different devices: /device:TPU:4 before, /device:TPU:24 now
where the time goes in v3:
time: 43.4 us; the launch traced here: 43.2 us
  Pallas kernels  42.6 us (98%)
  between operations  0.64 us (1%)
    pallas_call x1, Pallas kernels, local(): pl.pallas_call(kernel, out_shape=(pltpu.VMEM(queries.shape, BF16), pltpu....  40.9 us
    pallas_call x1, Pallas kernels, local(): pl.pallas_call(write_out, out_shape=[jax.ShapeDtypeStruct(g.shape, g.dtyp...  1.7 us

profile of v3, /device:TPU:24, one launch (start us, length us, event | category | flops | bytes accessed | tf_op | source)
XLA Modules:
  0.0 43.2 jit_solution(2420275977842511503)
XLA Ops:
  0.6 40.9 %shard_map.103 = (bf16[1,2,64,4096]{3,2,1,0:T(8,128)(2,1)S(1)}, f32[1,2,32,64]{3,2,1,0:T(8,128)S(1)}, bf16[1,8192,128]{2,1,0:T(8,128)(2,1)S(1)}) custom-call(s32[1,2]{1,0:T(1,128)} %slot_ref.1, s32[1,2]{1,0:T(1,128)} %doc_ref.1, f32[1,2,32,64]{3,2,1,0:T(8,128)} %bitcast.2, f32[1,2,64]{2,1,0:T(2,128)} %norm_ref.1, f32[1,2,64]{2,1,0:T(2,128)} %cot_ref.1, ...), custom_call_target="tpu_custom_call" | custom-call | tf_op jit(solution)/shard_map/pallas_call | solution.py:273
  41.5 1.7 %shard_map.104 = (bf16[1,2,64,4096]{3,2,1,0:T(8,128)(2,1)}, f32[1,2,32,64]{3,2,1,0:T(8,128)}, bf16[1,8192,128]{2,1,0:T(8,128)(2,1)}) custom-call(bf16[1,2,64,4096]{3,2,1,0:T(8,128)(2,1)S(1)} %get-tuple-element.9.refs_0_, f32[1,2,32,64]{3,2,1,0:T(8,128)S(1)} %get-tuple-element.10.refs_1_, bf16[1,8192,128]{2,1,0:T(8,128)(2,1)S(1)} %get-tuple-element.11.refs_2_), custom_call_target="tpu_custom_call" | custom-call | tf_op jit(solution)/shard_map/pallas_call | solution.py:310

commit v4 on v3

--- a/solution.py
+++ b/solution.py
@@ -14,7 +14,7 @@
 RIM = 3
 SLOTS = 4
 NT = 256
-CUT = 2
+CUT = 1
 PART = BLK // CUT
 LENT = RIM * CUT
 FACTOR = 1.0 / DH**0.5
@@ -96,18 +96,24 @@
                 parts.append(rows.astype(F32) * wide)
             both = jnp.concatenate(parts, axis=0).astype(BF16)
             qw_t[i][:, pair * 128 : (pair + 1) * 128] = both.T
+
+    barrier = pltpu.get_barrier_semaphore()
+
+    @pl.when(has_prev)
+    def _():
+        pl.semaphore_signal(barrier, inc=1, device_id={"ctx": prv}, device_id_type=MESH)
+
+    @pl.when(has_next)
+    def _():
+        pl.semaphore_signal(barrier, inc=1, device_id={"ctx": nxt}, device_id_type=MESH)
+
+    for i in range(TASKS):
         dk_v[i][SLOTS * CUT] = jnp.zeros((PART, DH), F32)
         u_v[i][...] = jnp.zeros((H * QT, DH), F32)
 
-    barrier = pltpu.get_barrier_semaphore()
-
-    @pl.when(has_prev)
-    def _():
-        pl.semaphore_signal(barrier, inc=1, device_id={"ctx": prv}, device_id_type=MESH)
-
-    @pl.when(has_next)
-    def _():
-        pl.semaphore_signal(barrier, inc=1, device_id={"ctx": nxt}, device_id_type=MESH)
+    @pl.when(jnp.logical_not(has_prev))
+    def _():
+        k_v[0:LENT] = jnp.zeros((LENT, PART, DH), BF16)
 
     pl.semaphore_wait(barrier, has_prev.astype(jnp.int32) + has_next.astype(jnp.int32))
 
@@ -178,10 +184,6 @@
             rim_copy(r).wait_recv()
             k_v[r] = rim_v[r]
 
-    @pl.when(jnp.logical_not(has_prev))
-    def _():
-        k_v[0:LENT] = jnp.zeros((LENT, PART, DH), BF16)
-
     for load in loads:
         load.wait()
 
@@ -254,10 +256,13 @@
             lend_copy(r).wait_send()
 
 
-def write_out(*refs):
-    copies = [
-        pltpu.make_async_copy(refs[j], refs[3 + j], refs[6].at[j]) for j in range(3)
-    ]
+def write_out(query_v, weight_v, key_v, query_hbm, weight_hbm, key_hbm, sem):
+    pairs = [(weight_v, weight_hbm)]
+    pairs += [(query_v.at[0, i], query_hbm.at[0, i]) for i in range(TASKS)]
+    for b in range(0, KB_DEV * BLK, 2 * BLK):
+        rows = pl.ds(b, 2 * BLK)
+        pairs.append((key_v.at[0, rows, :], key_hbm.at[0, rows, :]))
+    copies = [pltpu.make_async_copy(*pair, sem.at[j]) for j, pair in enumerate(pairs)]
     for copy in copies:
         copy.start()
     for copy in copies:
@@ -312,7 +317,7 @@
         out_shape=[jax.ShapeDtypeStruct(g.shape, g.dtype) for g in grads],
         in_specs=[vmem] * 3,
         out_specs=[hbm] * 3,
-        scratch_shapes=[dma((3,))],
+        scratch_shapes=[dma((1 + TASKS + KB_DEV // 2,))],
         compiler_params=pltpu.CompilerParams(vmem_limit_bytes=1 << 20),
     )(*[pltpu.with_memory_space_constraint(g, pltpu.VMEM) for g in grads])
     return query_grad, jnp.swapaxes(weight_grad, 2, 3), key_grad

time: 43.4 us -> 43.1 us (level)
  no operation moved by 1% of the time
where the time goes in v4:
time: 43.1 us; the launch traced here: 42.9 us
  Pallas kernels  42.3 us (98%)
  between operations  0.64 us (1%)
    pallas_call x1, Pallas kernels, local(): pl.pallas_call(kernel, out_shape=(pltpu.VMEM(queries.shape, BF16), pltpu....  40.5 us
    pallas_call x1, Pallas kernels, local(): pl.pallas_call(write_out, out_shape=[jax.ShapeDtypeStruct(g.shape, g.dtyp...  1.73 us

profile of v4, /device:TPU:24, one launch (start us, length us, event | category | flops | bytes accessed | tf_op | source)
XLA Modules:
  0.0 42.9 jit_solution(1054945256297458976)
XLA Ops:
  0.6 40.5 %shard_map.103 = (bf16[1,2,64,4096]{3,2,1,0:T(8,128)(2,1)S(1)}, f32[1,2,32,64]{3,2,1,0:T(8,128)S(1)}, bf16[1,8192,128]{2,1,0:T(8,128)(2,1)S(1)}) custom-call(s32[1,2]{1,0:T(1,128)} %slot_ref.1, s32[1,2]{1,0:T(1,128)} %doc_ref.1, f32[1,2,32,64]{3,2,1,0:T(8,128)} %bitcast.2, f32[1,2,64]{2,1,0:T(2,128)} %norm_ref.1, f32[1,2,64]{2,1,0:T(2,128)} %cot_ref.1, ...), custom_call_target="tpu_custom_call" | custom-call | tf_op jit(solution)/shard_map/pallas_call | solution.py:278
  41.2 1.7 %shard_map.104 = (bf16[1,2,64,4096]{3,2,1,0:T(8,128)(2,1)}, f32[1,2,32,64]{3,2,1,0:T(8,128)}, bf16[1,8192,128]{2,1,0:T(8,128)(2,1)}) custom-call(bf16[1,2,64,4096]{3,2,1,0:T(8,128)(2,1)S(1)} %get-tuple-element.9.query_v, f32[1,2,32,64]{3,2,1,0:T(8,128)S(1)} %get-tuple-element.10.weight_v, bf16[1,8192,128]{2,1,0:T(8,128)(2,1)S(1)} %get-tuple-element.11.key_v), custom_call_target="tpu_custom_call" | custom-call | tf_op jit(solution)/shard_map/pallas_call | solution.py:315

commit v5 on v4

--- a/solution.py
+++ b/solution.py
@@ -115,6 +115,8 @@
     def _():
         k_v[0:LENT] = jnp.zeros((LENT, PART, DH), BF16)
 
+    load_q.wait()
+    prepare(0)
     pl.semaphore_wait(barrier, has_prev.astype(jnp.int32) + has_next.astype(jnp.int32))
 
     @pl.when(has_next)
@@ -122,9 +124,7 @@
         for r in range(LENT):
             rim_copy(r).start()
 
-    load_q.wait()
-    for i in range(TASKS):
-        prepare(i)
+    prepare(1)
 
     def place(i, p):
         last = slot_ref[0, i] // (BLK // QT)

time: 43.1 us -> 43.1 us (level)
  no operation moved by 1% of the time
where the time goes in v5:
time: 43.1 us; the launch traced here: 42.9 us
  Pallas kernels  42.3 us (98%)
  between operations  0.64 us (1%)
    pallas_call x1, Pallas kernels, local(): pl.pallas_call(kernel, out_shape=(pltpu.VMEM(queries.shape, BF16), pltpu....  40.5 us
    pallas_call x1, Pallas kernels, local(): pl.pallas_call(write_out, out_shape=[jax.ShapeDtypeStruct(g.shape, g.dtyp...  1.73 us

profile of v5, /device:TPU:24, one launch (start us, length us, event | category | flops | bytes accessed | tf_op | source)
XLA Modules:
  0.0 42.9 jit_solution(3735643241584444806)
XLA Ops:
  0.6 40.5 %shard_map.103 = (bf16[1,2,64,4096]{3,2,1,0:T(8,128)(2,1)S(1)}, f32[1,2,32,64]{3,2,1,0:T(8,128)S(1)}, bf16[1,8192,128]{2,1,0:T(8,128)(2,1)S(1)}) custom-call(s32[1,2]{1,0:T(1,128)} %slot_ref.1, s32[1,2]{1,0:T(1,128)} %doc_ref.1, f32[1,2,32,64]{3,2,1,0:T(8,128)} %bitcast.2, f32[1,2,64]{2,1,0:T(2,128)} %norm_ref.1, f32[1,2,64]{2,1,0:T(2,128)} %cot_ref.1, ...), custom_call_target="tpu_custom_call" | custom-call | tf_op jit(solution)/shard_map/pallas_call | solution.py:278
  41.2 1.7 %shard_map.104 = (bf16[1,2,64,4096]{3,2,1,0:T(8,128)(2,1)}, f32[1,2,32,64]{3,2,1,0:T(8,128)}, bf16[1,8192,128]{2,1,0:T(8,128)(2,1)}) custom-call(bf16[1,2,64,4096]{3,2,1,0:T(8,128)(2,1)S(1)} %get-tuple-element.9.query_v, f32[1,2,32,64]{3,2,1,0:T(8,128)S(1)} %get-tuple-element.10.weight_v, bf16[1,8192,128]{2,1,0:T(8,128)(2,1)S(1)} %get-tuple-element.11.key_v), custom_call_target="tpu_custom_call" | custom-call | tf_op jit(solution)/shard_map/pallas_call | solution.py:315
